TPU v7x, 32 devices: a whole 2x2x4 slice. The times are simulated.
32 devices in a mesh: wide: 8 (over y, x, core), narrow: 4 (over z).
Axes of the slice: x: 2, y: 2, z: 4, core: 2. Of those that a mesh axis runs over, the one named last changes fastest.
Arguments:
- hamiltonian_tiles: float32 [12288, 6144], P('wide', 'narrow'), may hold values from -0.0546875 to 0.0546875
- row_columns: int32 [8, 4], P('wide'), may hold values from 0 to 7, as said below
- start_vectors: float32 [12288, 128], P(('wide', 'narrow')), may hold values from -60 to 60
Outputs:
- new_vectors: float32 [12288, 128], P(('wide', 'narrow'))
Inputs may be any that keep to these rules, and one draw needn't show every extreme that they name: For block row r = w + j // 4, row_columns[w, j] = (r + d) mod 8, with d = 0 where j % 4 = 0 and, for the other tiles of that block row, distinct d between 1 and 7; a block's mirror may also be stored.
All inputs are finite; a program needn't handle non-finite values.
Results may differ from a plain program's by a relative error of at most 0.0003.
Values sent between devices are 32-bit elements; how exact they have to be, the bound alone decides.
A program may use at most 64 MiB of HBM per device.

v0:
```python
import jax
import jax.numpy as jnp
from jax import lax
from jax.sharding import PartitionSpec as P

ITERS = 2
NS_STEPS = 5


def orthonormalize(product, gram, total_rows):
    width = gram.shape[0]
    identity = jnp.eye(width, dtype=jnp.float32)
    scale = jnp.sqrt(jnp.sum(gram * gram) + 1e-06)
    current = gram / scale
    inverse = identity
    for repeat in range(NS_STEPS):
        middle = 1.5 * identity - 0.5 * jnp.dot(inverse, current, precision=lax.Precision.HIGHEST)
        current = jnp.dot(current, middle, precision=lax.Precision.HIGHEST)
        inverse = jnp.dot(middle, inverse, precision=lax.Precision.HIGHEST)
    return jnp.dot(product, inverse, precision=lax.Precision.HIGHEST) * jnp.sqrt(total_rows / scale)


def on_device(hamiltonian_tiles, row_columns, start_vectors):
    narrow_count = lax.axis_size("narrow")
    wide_count = lax.axis_size("wide")
    my_index = lax.axis_index("narrow")
    order_tile = hamiltonian_tiles.shape[0]
    slice_rows = start_vectors.shape[0]
    width = start_vectors.shape[1]
    per_row = order_tile // slice_rows
    rows_group = narrow_count // per_row
    my_block = my_index // per_row
    columns_row = row_columns[0]
    column_group = columns_row // rows_group
    column_place = columns_row % rows_group
    my_column_place = column_place[my_index]
    sender_block = jnp.arange(narrow_count, dtype=jnp.int32) // per_row
    back_weight = (
        (column_group[:, None] == jnp.arange(wide_count, dtype=jnp.int32)[None, :])
        & (column_place[:, None] == my_block)
    ).astype(jnp.float32)
    own_weight = (sender_block == my_block).astype(jnp.float32)
    total_rows = float(wide_count * rows_group * order_tile)
    vectors = start_vectors
    for repeat in range(ITERS):
        slices = lax.all_gather(vectors, "wide", axis=0, tiled=True)
        picked = jnp.take(slices.reshape(wide_count, slice_rows, width), column_group, axis=0)
        gathered_rows = lax.all_gather(vectors, "narrow", axis=0, tiled=True)
        got_column = lax.all_to_all(picked, "narrow", split_axis=0, concat_axis=0, tiled=True)
        row_block = lax.dynamic_index_in_dim(
            gathered_rows.reshape(rows_group, order_tile, width), my_block, 0, keepdims=False
        )
        column_block = lax.dynamic_index_in_dim(
            got_column.reshape(rows_group, order_tile, width), my_column_place, 0, keepdims=False
        )
        direct = jnp.dot(hamiltonian_tiles, column_block, precision=lax.Precision.HIGHEST)
        transposed = lax.dot_general(
            hamiltonian_tiles, row_block, (((0,), (0,)), ((), ())), precision=lax.Precision.HIGHEST
        )
        transposed_spread = transposed.reshape(1, per_row, slice_rows, width).reshape(
            narrow_count, slice_rows, width
        )
        direct_spread = direct.reshape(1, per_row, slice_rows, width).reshape(
            narrow_count, slice_rows, width
        )
        arrived, direct_pieces = (
            lax.all_to_all(transposed_spread, "narrow", split_axis=0, concat_axis=0, tiled=True),
            lax.all_to_all(direct_spread, "narrow", split_axis=0, concat_axis=0, tiled=True),
        )
        direct_part = jnp.einsum(
            "n,nsk->sk", own_weight, direct_pieces, precision=lax.Precision.HIGHEST
        )
        placed = jnp.einsum("nb,nsk->bsk", back_weight, arrived, precision=lax.Precision.HIGHEST)
        moved_part = lax.psum_scatter(
            placed.reshape(wide_count * slice_rows, width), "wide", scatter_dimension=0, tiled=True
        )
        product = direct_part + moved_part
        local_gram = lax.dot_general(
            product, product, (((0,), (0,)), ((), ())), precision=lax.Precision.HIGHEST
        )
        gram = lax.psum(local_gram, ("wide", "narrow"))
        vectors = orthonormalize(product, gram, total_rows)
    return vectors


def solution(mesh):
    return jax.shard_map(
        on_device,
        mesh=mesh,
        in_specs=(P("wide", "narrow"), P("wide", None), P(("wide", "narrow"), None)),
        out_specs=P(("wide", "narrow"), None),
        check_vma=False,
    )
```

profile of v0, /device:TPU:1, one launch (start us, length us, event | category | flops | bytes accessed | tf_op | source)
XLA Modules:
  0.0 499.5 jit_solution(15545345940733565304)
XLA Ops:
  6.5 0.7 all-gather.3.cloned.1.call-update
  7.3 18.2 %all_gather.13 = f32[1536,128]{1,0:T(8,128)S(1)} all-gather(f32[384,128]{1,0:T(8,128)} %param.7), channel_id=1, replica_groups=mesh['wide'=8,'narrow'=4] {'narrow'}, dimensions={0}, use_global_device_ids=true | all-gather | bytes 983040 | tf_op jit(solution)/shard_map/all_gather | solution.py:48
  25.5 18.1 %fusion.41 = f32[1536,128]{1,0:T(8,128)} fusion(f32[1536,1536]{1,0:T(8,128)} %param.5, f32[1536,128]{1,0:T(8,128)S(1)} %all_gather.13), kind=kOutput, calls=%fused_computation.71 | convolution fusion | flops 3623878656 | bytes 11010048 | tf_op jit(solution)/shard_map/dot_general | solution.py:57
  43.6 4.0 all-to-all-start.2
  47.7 2.0 gather_fusion
  49.7 1.0 broadcast_select_fusion.1
  50.7 16.3 %all-to-all-done.2 = f32[4,384,128]{2,1,0:T(8,128)S(1)} async-done(((f32[4,384,128]{2,1,0:T(8,128)}), f32[4,384,128]{2,1,0:T(8,128)S(1)}, u32[]{:S(2)}, u32[]{:S(2)}) %all-to-all-start.2) | async-done | bytes 786464 | tf_op jit(solution)/shard_map/all_to_all | solution.py:67
  66.9 3.5 all-to-all-start
  70.5 1.5 fusion.12
  72.0 1.4 copy.12
  73.4 0.2 all-reduce.3.cloned.1.call-start
  73.6 16.4 %all-to-all-done = f32[4,384,128]{2,1,0:T(8,128)S(1)} async-done(((f32[4,384,128]{2,1,0:T(8,128)}), f32[4,384,128]{2,1,0:T(8,128)S(1)}, u32[]{:S(2)}, u32[]{:S(2)}) %all-to-all-start) | async-done | bytes 786464 | tf_op jit(solution)/shard_map/all_to_all | solution.py:49
  90.0 10.4 %fusion.40 = f32[128,1536]{1,0:T(8,128)S(1)} fusion(f32[1536,128]{1,0:T(8,128)S(1)} %bitcast.108, f32[1536,1536]{1,0:T(8,128)} %param.5), kind=kOutput, calls=%fused_computation.70 | convolution fusion | flops 3623878656 | bytes 11010048 | tf_op jit(solution)/shard_map/dot_general | solution.py:56
  100.5 21.5 %all_to_all.30 = f32[4,384,128]{1,2,0:T(8,128)S(1)} all-to-all(f32[4,384,128]{1,2,0:T(8,128)S(1)} %bitcast.106), channel_id=1, replica_groups=mesh['wide'=8,'narrow'=4] {'narrow'}, dimensions={0} | all-to-all | bytes 1572864 | tf_op jit(solution)/shard_map/all_to_all | solution.py:68
  122.1 0.3 copy.17
  122.4 0.8 fusion.20
  123.2 0.9 add.38
  124.2 1.1 fusion.42
  125.4 121.8 %all-reduce.3.cloned.1.call-done = f32[128,128]{1,0:T(8,128)} async-done(((f32[128,128]{1,0:T(8,128)}), f32[128,128]{1,0:T(8,128)}) %all-reduce.3.cloned.1.call-update) | async-done | bytes 65552 | tf_op jit(solution)/shard_map/psum | solution.py:81
  247.2 1.5 multiply_reduce_fusion.1
  249.3 1.0 fusion.9
  250.5 1.0 fusion.16
  251.6 0.2 fusion.8
  251.8 0.2 fusion.44
  252.0 0.2 fusion.43
  252.2 0.2 fusion.7
  252.4 0.2 fusion.46
  252.7 0.2 fusion.45
  252.9 0.2 fusion.6
  253.1 0.2 fusion.48
  253.3 0.2 fusion.47
  253.5 0.2 fusion.5
  254.0 1.0 convolution_multiply_fusion.1
  255.0 17.0 %all_gather.15 = f32[1536,128]{1,0:T(8,128)S(1)} all-gather(f32[384,128]{1,0:T(8,128)} %convolution_multiply_fusion.1), channel_id=1, replica_groups=mesh['wide'=8,'narrow'=4] {'narrow'}, dimensions={0}, use_global_device_ids=true | all-gather | bytes 983040 | tf_op jit(solution)/shard_map/all_gather | solution.py:48
  272.0 8.6 %convolution_bitcast_fusion = f32[1536,128]{0,1:T(8,128)S(1)} fusion(f32[1536,128]{1,0:T(8,128)S(1)} %all_gather.15, f32[1536,1536]{1,0:T(8,128)} %param.5), kind=kOutput, calls=%fused_computation.2 | convolution fusion | flops 3623878656 | bytes 11010048 | tf_op jit(solution)/shard_map/dot_general | solution.py:57
  280.6 1.1 copy.21
  281.7 4.1 all-to-all-start.5
  285.8 2.0 gather_fusion.1
  287.8 1.0 broadcast_select_fusion
  288.8 16.7 %all-to-all-done.5 = f32[4,384,128]{2,1,0:T(8,128)S(1)} async-done(((f32[4,384,128]{2,1,0:T(8,128)}), f32[4,384,128]{2,1,0:T(8,128)S(1)}, u32[]{:S(2)}, u32[]{:S(2)}) %all-to-all-start.5) | async-done | bytes 786464 | tf_op jit(solution)/shard_map/all_to_all | solution.py:67
  305.5 3.5 all-to-all-start.3
  309.0 0.3 reduce-scatter.5.cloned.1.call-start
  309.3 1.5 fusion.10
  310.7 1.4 copy.16
  312.2 16.4 %all-to-all-done.3 = f32[4,384,128]{2,1,0:T(8,128)S(1)} async-done(((f32[4,384,128]{2,1,0:T(8,128)}), f32[4,384,128]{2,1,0:T(8,128)S(1)}, u32[]{:S(2)}, u32[]{:S(2)}) %all-to-all-start.3) | async-done | bytes 786464 | tf_op jit(solution)/shard_map/all_to_all | solution.py:49
  328.6 10.4 %fusion.50 = f32[128,1536]{1,0:T(8,128)S(1)} fusion(f32[1536,128]{1,0:T(8,128)S(1)} %bitcast.109, f32[1536,1536]{1,0:T(8,128)} %param.5), kind=kOutput, calls=%fused_computation.80 | convolution fusion | flops 3623878656 | bytes 11010048 | tf_op jit(solution)/shard_map/dot_general | solution.py:56
  339.1 21.5 %all_to_all.31 = f32[4,384,128]{1,2,0:T(8,128)S(1)} all-to-all(f32[4,384,128]{1,2,0:T(8,128)S(1)} %bitcast.107), channel_id=1, replica_groups=mesh['wide'=8,'narrow'=4] {'narrow'}, dimensions={0} | all-to-all | bytes 1572864 | tf_op jit(solution)/shard_map/all_to_all | solution.py:68
  360.6 0.3 copy.19
  361.0 0.8 fusion.22
  361.8 0.9 add.40
  362.8 1.1 fusion.51
  363.9 120.9 %all-reduce.5.cloned.1.call-done = f32[128,128]{1,0:T(8,128)} async-done(((f32[128,128]{1,0:T(8,128)}), f32[128,128]{1,0:T(8,128)}) %all-reduce.5.cloned.1.call-update) | async-done | bytes 65552 | tf_op jit(solution)/shard_map/psum | solution.py:81
  484.8 1.5 multiply_reduce_fusion
  487.0 1.0 fusion.4
  488.2 1.0 fusion.17
  489.3 0.2 fusion.3
  489.5 0.2 fusion.53
  489.9 0.2 fusion.2
  490.5 0.2 fusion.1
  490.7 0.2 fusion.57
  491.0 0.2 fusion.56
  491.2 0.2 fusion
  491.4 0.2 fusion.58
  491.7 1.0 convolution_multiply_fusion
  (26 shorter events, 1.6 us)
Async XLA Ops:
  6.5 41.1 %all-gather.3.cloned.1.call-start = ((), (), s32[]{:S(2)}) async-start(), calls=%async_computation.8 | async-start | bytes 1769472 | tf_op jit(solution)/shard_map/all_gather | solution.py:46
  25.5 22.1 %copy-start = (s32[1,4]{1,0:T(1,128)S(1)}, s32[1,4]{1,0:T(1,128)}, u32[]{:S(2)}) copy-start(s32[1,4]{1,0:T(1,128)} %param.6) | copy-start | bytes 52
  43.6 23.4 %all-to-all-start.2 = ((f32[4,384,128]{2,1,0:T(8,128)}), f32[4,384,128]{2,1,0:T(8,128)S(1)}, u32[]{:S(2)}, u32[]{:S(2)}) async-start(f32[4,384,128]{2,1,0:T(8,128)} %bitcast.9), calls=%async_computation.2 | async-start | bytes 1572864 | tf_op jit(solution)/shard_map/all_to_all | solution.py:67
  66.9 23.1 %all-to-all-start = ((f32[4,384,128]{2,1,0:T(8,128)}), f32[4,384,128]{2,1,0:T(8,128)S(1)}, u32[]{:S(2)}, u32[]{:S(2)}) async-start(f32[4,384,128]{2,1,0:T(8,128)} %broadcast_select_fusion.1), calls=%async_computation | async-start | bytes 1572864 | tf_op jit(solution)/shard_map/all_to_all | solution.py:49
  70.4 52.8 %reduce-scatter.3.cloned.1.call-start = ((), (), s32[]{:S(2)}) async-start(), calls=%async_computation.9 | async-start | bytes 1769472 | tf_op jit(solution)/shard_map/reduce_scatter | solution.py:74
  73.4 173.8 %all-reduce.3.cloned.1.call-start = ((), (), s32[]{:S(2)}) async-start(), calls=%async_computation.10 | async-start | bytes 131072 | tf_op jit(solution)/shard_map/psum | solution.py:81
  125.3 160.5 %all-gather.5.cloned.1.call-start = ((), (), s32[]{:S(2)}) async-start(), calls=%async_computation.11 | async-start | bytes 1769472 | tf_op jit(solution)/shard_map/all_gather | solution.py:46
  281.7 23.8 %all-to-all-start.5 = ((f32[4,384,128]{2,1,0:T(8,128)}), f32[4,384,128]{2,1,0:T(8,128)S(1)}, u32[]{:S(2)}, u32[]{:S(2)}) async-start(f32[4,384,128]{2,1,0:T(8,128)} %bitcast.17), calls=%async_computation.6 | async-start | bytes 1572864 | tf_op jit(solution)/shard_map/all_to_all | solution.py:67
  305.5 23.1 %all-to-all-start.3 = ((f32[4,384,128]{2,1,0:T(8,128)}), f32[4,384,128]{2,1,0:T(8,128)S(1)}, u32[]{:S(2)}, u32[]{:S(2)}) async-start(f32[4,384,128]{2,1,0:T(8,128)} %broadcast_select_fusion), calls=%async_computation.4 | async-start | bytes 1572864 | tf_op jit(solution)/shard_map/all_to_all | solution.py:49
  309.0 52.8 %reduce-scatter.5.cloned.1.call-start = ((), (), s32[]{:S(2)}) async-start(), calls=%async_computation.12 | async-start | bytes 1769472 | tf_op jit(solution)/shard_map/reduce_scatter | solution.py:74
  312.2 172.6 %all-reduce.5.cloned.1.call-start = ((), (), s32[]{:S(2)}) async-start(), calls=%async_computation.13 | async-start | bytes 131072 | tf_op jit(solution)/shard_map/psum | solution.py:81
Sparse Core Ops, SparseCore 0:
  9.2 28.0 all-gather.2
  74.5 40.6 reduce-scatter.2
  125.5 121.6 all-reduce.2
  255.1 25.3 all-gather.4
  312.8 39.4 reduce-scatter.4
  364.0 120.7 all-reduce.4
where the time goes:
time: 500 us
  waiting for transfers between devices  309 us (62%)
  blocking collectives  78.3 us (16%)
  matrix products  65.2 us (13%)
  starting transfers between devices  15.8 us (3%)
  between operations  15.4 us (3%)
  local copies, waits for them, and re-layouts  8.74 us (2%)
  other arithmetic  6.83 us (1%)
    psum x2, waiting for transfers between devices, on_device(): gram = lax.psum(local_gram, ('wide', 'narrow'))  243 us
    all_to_all x2, blocking collectives, on_device(): lax.all_to_all(direct_spread, 'narrow', split_axis=0, concat_axis=0, tile...  43.1 us
    all_gather x2, blocking collectives, on_device(): gathered_rows = lax.all_gather(vectors, 'narrow', axis=0, tiled=True)  35.2 us
    all_to_all x2, waiting for transfers between devices, on_device(): lax.all_to_all(transposed_spread, 'narrow', split_axis=0, concat_axis=0,...  32.9 us
    all_to_all x2, waiting for transfers between devices, on_device(): lax.all_to_all(picked, 'narrow', split_axis=0, concat_axis=0, tiled=True)  32.8 us
    dot_general x2, matrix products, on_device(): lax.dot_general(hamiltonian_tiles, row_block, (((0,), (0,)), ((), ())), p...  26.6 us
    dot_general x2, matrix products, on_device(): jnp.dot(hamiltonian_tiles, column_block, precision=lax.Precision.HIGHEST)  20.9 us
  transfers between devices with their start and end apart: 10, of which 6 were waited for; matrix products, arithmetic and copies ran while one was open for 13% of the time, Pallas kernels for 0%

commit v1 on v0

--- a/solution.py
+++ b/solution.py
@@ -78,7 +78,8 @@
         local_gram = lax.dot_general(
             product, product, (((0,), (0,)), ((), ())), precision=lax.Precision.HIGHEST
         )
-        gram = lax.psum(local_gram, ("wide", "narrow"))
+        one_axis = lax.psum(local_gram, "narrow")
+        gram = lax.psum(one_axis, "wide")
         vectors = orthonormalize(product, gram, total_rows)
     return vectors
 

time: 500 us -> 433 us (0.87)
  waiting for transfers between devices: 309 us -> 242 us
    psum x2 -> x4, waiting for transfers between devices: 243 us -> 178 us  [the longest x2 114 us: on_device(): gram = lax.psum(one_axis, 'wide')]
  transfers between devices with their start and end apart: 10 -> 12, of which waited for: 6 -> 8; matrix products, arithmetic and copies ran while one was open for 13% -> 15% of each run, Pallas kernels for 0% -> 0%
where the time goes in v1:
time: 433 us; the launch traced here: 431 us
  waiting for transfers between devices  242 us (56%)
  blocking collectives  77.1 us (18%)
  matrix products  65 us (15%)
  starting transfers between devices  16 us (4%)
  between operations  15.5 us (4%)
  local copies, waits for them, and re-layouts  8.74 us (2%)
  other arithmetic  6.83 us (2%)
    psum x2, waiting for transfers between devices, on_device(): gram = lax.psum(one_axis, 'wide')  114 us
    psum x2, waiting for transfers between devices, on_device(): one_axis = lax.psum(local_gram, 'narrow')  64.2 us
    all_to_all x2, blocking collectives, on_device(): lax.all_to_all(direct_spread, 'narrow', split_axis=0, concat_axis=0, tile...  43 us
    all_gather x2, blocking collectives, on_device(): gathered_rows = lax.all_gather(vectors, 'narrow', axis=0, tiled=True)  34.1 us
    all_to_all x2, waiting for transfers between devices, on_device(): lax.all_to_all(picked, 'narrow', split_axis=0, concat_axis=0, tiled=True)  31.8 us
    all_to_all x2, waiting for transfers between devices, on_device(): lax.all_to_all(transposed_spread, 'narrow', split_axis=0, concat_axis=0,...  30.6 us
    dot_general x2, matrix products, on_device(): lax.dot_general(hamiltonian_tiles, row_block, (((0,), (0,)), ((), ())), p...  26.4 us
    dot_general x2, matrix products, on_device(): jnp.dot(hamiltonian_tiles, column_block, precision=lax.Precision.HIGHEST)  20.9 us
  transfers between devices with their start and end apart: 12, of which 8 were waited for; matrix products, arithmetic and copies ran while one was open for 15% of the time, Pallas kernels for 0%

profile of v1, /device:TPU:1, one launch (start us, length us, event | category | flops | bytes accessed | tf_op | source)
XLA Modules:
  0.0 430.8 jit_solution(5624447132639914177)
XLA Ops:
  6.5 0.7 all-gather.3.cloned.1.call-update
  7.3 18.2 %all_gather.13 = f32[1536,128]{1,0:T(8,128)S(1)} all-gather(f32[384,128]{1,0:T(8,128)} %param.7), channel_id=1, replica_groups=mesh['wide'=8,'narrow'=4] {'narrow'}, dimensions={0}, use_global_device_ids=true | all-gather | bytes 983040 | tf_op jit(solution)/shard_map/all_gather | solution.py:48
  25.5 18.1 %fusion.41 = f32[1536,128]{1,0:T(8,128)} fusion(f32[1536,1536]{1,0:T(8,128)} %param.5, f32[1536,128]{1,0:T(8,128)S(1)} %all_gather.13), kind=kOutput, calls=%fused_computation.71 | convolution fusion | flops 3623878656 | bytes 11010048 | tf_op jit(solution)/shard_map/dot_general | solution.py:57
  43.6 4.0 all-to-all-start.2
  47.7 2.0 gather_fusion
  49.7 1.0 broadcast_select_fusion.1
  50.7 16.3 %all-to-all-done.2 = f32[4,384,128]{2,1,0:T(8,128)S(1)} async-done(((f32[4,384,128]{2,1,0:T(8,128)}), f32[4,384,128]{2,1,0:T(8,128)S(1)}, u32[]{:S(2)}, u32[]{:S(2)}) %all-to-all-start.2) | async-done | bytes 786464 | tf_op jit(solution)/shard_map/all_to_all | solution.py:67
  66.9 3.5 all-to-all-start
  70.5 1.5 fusion.12
  72.0 1.4 copy.12
  73.4 0.2 all-reduce.5.cloned.1.call-start
  73.6 16.4 %all-to-all-done = f32[4,384,128]{2,1,0:T(8,128)S(1)} async-done(((f32[4,384,128]{2,1,0:T(8,128)}), f32[4,384,128]{2,1,0:T(8,128)S(1)}, u32[]{:S(2)}, u32[]{:S(2)}) %all-to-all-start) | async-done | bytes 786464 | tf_op jit(solution)/shard_map/all_to_all | solution.py:49
  90.0 10.4 %fusion.40 = f32[128,1536]{1,0:T(8,128)S(1)} fusion(f32[1536,128]{1,0:T(8,128)S(1)} %bitcast.108, f32[1536,1536]{1,0:T(8,128)} %param.5), kind=kOutput, calls=%fused_computation.70 | convolution fusion | flops 3623878656 | bytes 11010048 | tf_op jit(solution)/shard_map/dot_general | solution.py:56
  100.5 21.5 %all_to_all.30 = f32[4,384,128]{1,2,0:T(8,128)S(1)} all-to-all(f32[4,384,128]{1,2,0:T(8,128)S(1)} %bitcast.106), channel_id=1, replica_groups=mesh['wide'=8,'narrow'=4] {'narrow'}, dimensions={0} | all-to-all | bytes 1572864 | tf_op jit(solution)/shard_map/all_to_all | solution.py:68
  122.1 0.3 copy.17
  122.4 0.8 fusion.20
  123.2 0.9 add.42
  124.2 1.1 fusion.42
  125.4 32.8 %all-reduce.5.cloned.1.call-done = f32[128,128]{1,0:T(8,128)} async-done(((f32[128,128]{1,0:T(8,128)}), f32[128,128]{1,0:T(8,128)}) %all-reduce.5.cloned.1.call-update) | async-done | bytes 65552 | tf_op jit(solution)/shard_map/psum | solution.py:81
  158.2 57.0 %all-reduce.7.cloned.1.call-done = f32[128,128]{1,0:T(8,128)} async-done(((f32[128,128]{1,0:T(8,128)}), f32[128,128]{1,0:T(8,128)}) %all-reduce.7.cloned.1.call-update) | async-done | bytes 65552 | tf_op jit(solution)/shard_map/psum | solution.py:82
  215.2 1.5 multiply_reduce_fusion.1
  217.4 1.0 fusion.9
  218.6 1.0 fusion.16
  219.6 0.2 fusion.8
  220.3 0.2 fusion.7
  220.5 0.2 fusion.46
  220.7 0.2 fusion.45
  220.9 0.2 fusion.6
  221.3 0.2 fusion.47
  221.6 0.2 fusion.5
  221.8 0.2 fusion.49
  222.1 1.0 convolution_multiply_fusion.1
  223.1 15.8 %all_gather.15 = f32[1536,128]{1,0:T(8,128)S(1)} all-gather(f32[384,128]{1,0:T(8,128)} %convolution_multiply_fusion.1), channel_id=1, replica_groups=mesh['wide'=8,'narrow'=4] {'narrow'}, dimensions={0}, use_global_device_ids=true | all-gather | bytes 983040 | tf_op jit(solution)/shard_map/all_gather | solution.py:48
  238.9 8.3 %convolution_bitcast_fusion = f32[1536,128]{0,1:T(8,128)S(1)} fusion(f32[1536,128]{1,0:T(8,128)S(1)} %all_gather.15, f32[1536,1536]{1,0:T(8,128)} %param.5), kind=kOutput, calls=%fused_computation.2 | convolution fusion | flops 3623878656 | bytes 11010048 | tf_op jit(solution)/shard_map/dot_general | solution.py:57
  247.2 1.1 copy.21
  248.4 4.3 all-to-all-start.5
  252.6 2.0 gather_fusion.1
  254.7 1.0 broadcast_select_fusion
  255.7 14.4 %all-to-all-done.5 = f32[4,384,128]{2,1,0:T(8,128)S(1)} async-done(((f32[4,384,128]{2,1,0:T(8,128)}), f32[4,384,128]{2,1,0:T(8,128)S(1)}, u32[]{:S(2)}, u32[]{:S(2)}) %all-to-all-start.5) | async-done | bytes 786464 | tf_op jit(solution)/shard_map/all_to_all | solution.py:67
  270.0 3.5 all-to-all-start.3
  273.5 0.3 reduce-scatter.5.cloned.1.call-start
  273.8 1.5 fusion.10
  275.3 1.4 copy.16
  276.8 15.4 %all-to-all-done.3 = f32[4,384,128]{2,1,0:T(8,128)S(1)} async-done(((f32[4,384,128]{2,1,0:T(8,128)}), f32[4,384,128]{2,1,0:T(8,128)S(1)}, u32[]{:S(2)}, u32[]{:S(2)}) %all-to-all-start.3) | async-done | bytes 786464 | tf_op jit(solution)/shard_map/all_to_all | solution.py:49
  292.1 10.5 %fusion.50 = f32[128,1536]{1,0:T(8,128)S(1)} fusion(f32[1536,128]{1,0:T(8,128)S(1)} %bitcast.109, f32[1536,1536]{1,0:T(8,128)} %param.5), kind=kOutput, calls=%fused_computation.80 | convolution fusion | flops 3623878656 | bytes 11010048 | tf_op jit(solution)/shard_map/dot_general | solution.py:56
  302.7 21.5 %all_to_all.31 = f32[4,384,128]{1,2,0:T(8,128)S(1)} all-to-all(f32[4,384,128]{1,2,0:T(8,128)S(1)} %bitcast.107), channel_id=1, replica_groups=mesh['wide'=8,'narrow'=4] {'narrow'}, dimensions={0} | all-to-all | bytes 1572864 | tf_op jit(solution)/shard_map/all_to_all | solution.py:68
  324.1 0.3 copy.19
  324.5 0.8 fusion.22
  325.3 0.9 add.44
  326.3 1.1 fusion.51
  327.5 31.4 %all-reduce.9.cloned.1.call-done = f32[128,128]{1,0:T(8,128)} async-done(((f32[128,128]{1,0:T(8,128)}), f32[128,128]{1,0:T(8,128)}) %all-reduce.9.cloned.1.call-update) | async-done | bytes 65552 | tf_op jit(solution)/shard_map/psum | solution.py:81
  358.9 57.2 %all-reduce.11.cloned.1.call-done = f32[128,128]{1,0:T(8,128)} async-done(((f32[128,128]{1,0:T(8,128)}), f32[128,128]{1,0:T(8,128)}) %all-reduce.11.cloned.1.call-update) | async-done | bytes 65552 | tf_op jit(solution)/shard_map/psum | solution.py:82
  416.1 1.5 multiply_reduce_fusion
  418.2 1.0 fusion.4
  419.5 1.0 fusion.17
  420.5 0.2 fusion.3
  420.9 0.2 fusion.52
  421.1 0.2 fusion.2
  421.4 0.2 fusion.55
  421.6 0.2 fusion.54
  421.8 0.2 fusion.1
  422.5 0.2 fusion
  422.7 0.2 fusion.58
  422.9 1.0 convolution_multiply_fusion
  (32 shorter events, 2.1 us)
Async XLA Ops:
  6.5 41.1 %all-gather.3.cloned.1.call-start = ((), (), s32[]{:S(2)}) async-start(), calls=%async_computation.8 | async-start | bytes 1769472 | tf_op jit(solution)/shard_map/all_gather | solution.py:46
  25.5 22.1 %copy-start = (s32[1,4]{1,0:T(1,128)S(1)}, s32[1,4]{1,0:T(1,128)}, u32[]{:S(2)}) copy-start(s32[1,4]{1,0:T(1,128)} %param.6) | copy-start | bytes 52
  43.6 23.4 %all-to-all-start.2 = ((f32[4,384,128]{2,1,0:T(8,128)}), f32[4,384,128]{2,1,0:T(8,128)S(1)}, u32[]{:S(2)}, u32[]{:S(2)}) async-start(f32[4,384,128]{2,1,0:T(8,128)} %bitcast.9), calls=%async_computation.2 | async-start | bytes 1572864 | tf_op jit(solution)/shard_map/all_to_all | solution.py:67
  66.9 23.1 %all-to-all-start = ((f32[4,384,128]{2,1,0:T(8,128)}), f32[4,384,128]{2,1,0:T(8,128)S(1)}, u32[]{:S(2)}, u32[]{:S(2)}) async-start(f32[4,384,128]{2,1,0:T(8,128)} %broadcast_select_fusion.1), calls=%async_computation | async-start | bytes 1572864 | tf_op jit(solution)/shard_map/all_to_all | solution.py:49
  70.4 52.8 %reduce-scatter.3.cloned.1.call-start = ((), (), s32[]{:S(2)}) async-start(), calls=%async_computation.9 | async-start | bytes 1769472 | tf_op jit(solution)/shard_map/reduce_scatter | solution.py:74
  73.4 84.7 %all-reduce.5.cloned.1.call-start = ((), (), s32[]{:S(2)}) async-start(), calls=%async_computation.10 | async-start | bytes 131072 | tf_op jit(solution)/shard_map/psum | solution.py:81
  125.3 89.9 %all-reduce.7.cloned.1.call-start = ((), (), s32[]{:S(2)}) async-start(), calls=%async_computation.11 | async-start | bytes 131072 | tf_op jit(solution)/shard_map/psum | solution.py:82
  158.2 94.5 %all-gather.5.cloned.1.call-start = ((), (), s32[]{:S(2)}) async-start(), calls=%async_computation.12 | async-start | bytes 1769472 | tf_op jit(solution)/shard_map/all_gather | solution.py:46
  248.4 21.7 %all-to-all-start.5 = ((f32[4,384,128]{2,1,0:T(8,128)}), f32[4,384,128]{2,1,0:T(8,128)S(1)}, u32[]{:S(2)}, u32[]{:S(2)}) async-start(f32[4,384,128]{2,1,0:T(8,128)} %bitcast.17), calls=%async_computation.6 | async-start | bytes 1572864 | tf_op jit(solution)/shard_map/all_to_all | solution.py:67
  270.0 22.1 %all-to-all-start.3 = ((f32[4,384,128]{2,1,0:T(8,128)}), f32[4,384,128]{2,1,0:T(8,128)S(1)}, u32[]{:S(2)}, u32[]{:S(2)}) async-start(f32[4,384,128]{2,1,0:T(8,128)} %broadcast_select_fusion), calls=%async_computation.4 | async-start | bytes 1572864 | tf_op jit(solution)/shard_map/all_to_all | solution.py:49
  273.5 51.8 %reduce-scatter.5.cloned.1.call-start = ((), (), s32[]{:S(2)}) async-start(), calls=%async_computation.13 | async-start | bytes 1769472 | tf_op jit(solution)/shard_map/reduce_scatter | solution.py:74
  276.7 82.1 %all-reduce.9.cloned.1.call-start = ((), (), s32[]{:S(2)}) async-start(), calls=%async_computation.14 | async-start | bytes 131072 | tf_op jit(solution)/shard_map/psum | solution.py:81
  327.4 88.7 %all-reduce.11.cloned.1.call-start = ((), (), s32[]{:S(2)}) async-start(), calls=%async_computation.15 | async-start | bytes 131072 | tf_op jit(solution)/shard_map/psum | solution.py:82
Sparse Core Ops, SparseCore 0:
  9.2 28.0 all-gather.2
  74.5 40.6 reduce-scatter.2
  125.5 32.6 all-reduce.4
  161.1 54.1 all-reduce.6
  223.2 26.1 all-gather.4
  277.3 40.9 reduce-scatter.4
  327.5 31.2 all-reduce.8
  361.9 54.1 all-reduce.10
